TPU v7x, 256 devices: a whole 4x4x8 slice. The times are simulated.
256 devices in a mesh: sec: 32 (over z, y), blk: 8 (over x, core).
Axes of the slice: x: 4, y: 4, z: 8, core: 2. Of those that a mesh axis runs over, the one named last changes fastest.
Arguments:
- state_now: float32 [128, 65536], P(None, ('sec', 'blk')), may hold values from -5 to 5
- source: float32 [128, 65536], P(None, ('sec', 'blk')), may hold values from -6 to 6
- fan_gain: float32 [65536], P(('sec', 'blk')), may hold values from 0.5 to 12
- section_block: bfloat16 [65536, 2048], P(('sec', 'blk')), may hold values from -1 to 7
- block_inverse: bfloat16 [65536, 2048], P(('sec', 'blk')), may hold values from -1 to 1
- back_panel: bfloat16 [65536, 128], P(('sec', 'blk')), may hold values from -6 to 6
- ahead_panel: bfloat16 [65536, 128], P(('sec', 'blk')), may hold values from -0.0625 to 0.0625
- interface: int32 [32, 128], P('sec'), may hold values from 0 to 2047, as said below
Outputs:
- new_state: float32 [128, 65536], P(None, ('sec', 'blk'))
Inputs may be any that keep to these rules, and one draw needn't show every extreme that they name: `interface`: entries of one section are distinct; entry p lies in [p * 16, (p + 1) * 16).
All inputs are finite; a program needn't handle non-finite values.
Results may differ from a plain program's by a relative error of at most 0.0063.
Values may be sent and summed in bfloat16 or wider, within the bound.
A program may use at most 64 MiB of HBM per device.

v0:
```python
import jax
import jax.numpy as jnp
from jax import lax
from jax.sharding import PartitionSpec as P

KRYLOV = 3
epsilon = 1e-06


def extended(x, sides, width):
    for axis, dim in sides:
        size, length = (lax.axis_size(axis), x.shape[dim])
        up = [(i, (i + 1) % size) for i in range(size - 1)]
        down = [(j, i) for i, j in up]
        last = lax.slice_in_dim(x, length - width, length, axis=dim)
        first = lax.slice_in_dim(x, 0, width, axis=dim)
        before = lax.ppermute(last, axis, up)
        after = lax.ppermute(first, axis, down)
        x = jnp.concatenate([before, x, after], axis=dim)
    return x


def entering(value, axis, join, neutral):
    count, mine = (lax.axis_size(axis), lax.axis_index(axis))
    pieces = jax.tree.map(lambda part: lax.all_gather(part, axis), value)
    so_far = jax.tree.map(
        lambda part, zero: jnp.full_like(part, 0) + jnp.asarray(zero, part.dtype), value, neutral
    )

    def step(position, so_far):
        longer = join(so_far, jax.tree.map(lambda part: part[position], pieces))
        return jax.tree.map(lambda new, old: jnp.where(position < mine, new, old), longer, so_far)

    return lax.fori_loop(0, count - 1, step, so_far)


def least_squares(hessen, beta):
    cases = hessen.shape[0]
    depth = hessen.shape[2]
    rhs = jnp.zeros((cases, depth + 1), jnp.float32).at[:, 0].set(beta)
    upper = hessen
    for column in range(depth):
        upper_row = upper[:, column, :]
        lower_row = upper[:, column + 1, :]
        radius = jnp.sqrt(upper_row[:, column] ** 2 + lower_row[:, column] ** 2)
        cosine = upper_row[:, column] / radius
        sine_term = lower_row[:, column] / radius
        upper = upper.at[:, column, :].set(
            cosine[:, None] * upper_row + sine_term[:, None] * lower_row
        )
        upper = upper.at[:, column + 1, :].set(
            -sine_term[:, None] * upper_row + cosine[:, None] * lower_row
        )
        first_rhs = rhs[:, column]
        second_rhs = rhs[:, column + 1]
        rhs = rhs.at[:, column].set(cosine * first_rhs + sine_term * second_rhs)
        rhs = rhs.at[:, column + 1].set(-sine_term * first_rhs + cosine * second_rhs)
    weights = jnp.zeros((cases, depth), jnp.float32)
    for column in reversed(range(depth)):
        remain = rhs[:, column] - jnp.sum(
            upper[:, column, column + 1 :] * weights[:, column + 1 :], axis=1
        )
        weights = weights.at[:, column].set(remain / upper[:, column, column])
    return weights


def local(
    state_now, source, fan_gain, section_block, block_inverse, back_panel, ahead_panel, interface
):
    highest = lax.Precision.HIGHEST
    cases, node_rows = state_now.shape
    panel_width = back_panel.shape[1]
    indices = interface[0]
    first_row = lax.axis_index("blk") * node_rows
    selector = (indices[None, :] == first_row + jnp.arange(node_rows)[:, None]).astype(jnp.float32)
    contract = (((1,), (1,)), ((), ()))
    gain_panel = jnp.dot(
        block_inverse,
        lax.all_gather(back_panel, "blk", axis=0, tiled=True),
        preferred_element_type=jnp.float32,
    )
    panel_maps = -lax.psum(jnp.dot(selector.T, gain_panel, precision=highest), "blk")

    def section_terms(dense_part, behind_vals, piece):
        width = piece.shape[1]
        dense_part = lax.dot_general(
            piece, section_block, contract, preferred_element_type=jnp.float32
        )
        picker = (indices[None, :] == jnp.arange(width)[:, None]).astype(jnp.bfloat16)
        behind_vals = jnp.dot(piece, picker, preferred_element_type=jnp.float32)
        return (dense_part, behind_vals)

    def fold_section(carry, piece):
        return section_terms(carry[0], carry[1], piece)

    def operator(vector):
        rounded = vector.astype(jnp.bfloat16)
        empty_dense = jnp.zeros((cases, node_rows), jnp.float32)
        empty_panel = jnp.zeros((cases, panel_width), jnp.float32)
        start_carry = (empty_dense, empty_panel)
        folded = fold_section(start_carry, lax.all_gather(rounded, "blk", axis=1, tiled=True))
        dense_part, behind_vals = folded
        upward = lax.psum(jnp.dot(rounded, ahead_panel, preferred_element_type=jnp.float32), "blk")
        framed = extended(jnp.stack([behind_vals, upward])[None], (("sec", 0),), 1)
        behind = framed[0, 0].astype(jnp.bfloat16)
        ahead_term = framed[2, 1]
        lower_term = lax.dot_general(
            behind, back_panel, contract, preferred_element_type=jnp.float32
        )
        upper_term = jnp.dot(ahead_term, selector.T, precision=highest)
        return dense_part + lower_term + upper_term

    def compose(earlier, later):
        first_map, first_value = earlier
        second_map, second_value = later
        joined_map = jnp.dot(second_map, first_map, precision=highest)
        joined_value = jnp.dot(first_value, second_map.T, precision=highest) + second_value
        return (joined_map, joined_value)

    def lengths(vector):
        return jnp.sqrt(lax.psum(jnp.sum(vector * vector, axis=1), ("sec", "blk")) + epsilon)

    bent = jnp.tanh(state_now)
    residual = source - operator(state_now) - fan_gain[None, :] * bent
    jac_diag = fan_gain[None, :] * (1.0 - bent * bent)
    beta = lengths(residual)
    basis = [residual / beta[:, None]]
    directions = []
    hessen = jnp.zeros((cases, KRYLOV + 1, KRYLOV), jnp.float32)
    for column in range(KRYLOV):
        precondition_rounded = basis[column].astype(jnp.bfloat16)
        precondition_folded = lax.dot_general(
            lax.all_gather(precondition_rounded, "blk", axis=1, tiled=True),
            block_inverse,
            contract,
            preferred_element_type=jnp.float32,
        )
        values = lax.psum(jnp.dot(precondition_folded, selector, precision=highest), "blk")
        identity = (
            jnp.eye(panel_width, dtype=jnp.float32),
            jnp.zeros((cases, panel_width), jnp.float32),
        )
        _, before = entering((panel_maps, values), "sec", compose, identity)
        direction = precondition_folded - lax.dot_general(
            before, gain_panel, contract, precision=highest
        )
        product = operator(direction) + jac_diag * direction
        stacked = jnp.stack(basis)
        projections = lax.psum(jnp.sum(product[None] * stacked, axis=2), ("sec", "blk"))
        product = product - jnp.sum(projections[:, :, None] * stacked, axis=0)
        length = lengths(product)
        hessen = hessen.at[:, : column + 1, column].set(projections.T)
        hessen = hessen.at[:, column + 1, column].set(length)
        basis.append(product / length[:, None])
        directions.append(direction)
    weights = least_squares(hessen, beta)
    update = jnp.zeros_like(state_now)
    for column in range(KRYLOV):
        update = update + weights[:, column : column + 1] * directions[column]
    return state_now + update


def solution(mesh):
    in_specs = (
        P(None, ("sec", "blk")),
        P(None, ("sec", "blk")),
        P(("sec", "blk")),
        P(("sec", "blk"), None),
        P(("sec", "blk"), None),
        P(("sec", "blk"), None),
        P(("sec", "blk"), None),
        P("sec", None),
    )
    out_specs = P(None, ("sec", "blk"))
    return jax.shard_map(local, mesh=mesh, in_specs=in_specs, out_specs=out_specs, check_vma=False)
```

profile of v0, /device:TPU:1, one launch (start us, length us, event | category | flops | bytes accessed | tf_op | source)
XLA Modules:
  0.0 1640.1 jit_solution(12427240941463223437)
XLA Ops:
  40.7 34.6 %all-reduce.11.cloned.1.call-done = f32[1,128,128]{1,2,0:T(8,128)} async-done(((f32[1,128,128]{1,2,0:T(8,128)}), f32[1,128,128]{1,2,0:T(8,128)}) %all-reduce.11.cloned.1.call-update) | async-done | bytes 65552 | tf_op jit(solution)/shard_map/psum | solution.py:103
  86.3 83.2 %psum.106 = f32[128]{0:T(128)S(1)} all-reduce(f32[128]{0:T(128)S(1)} %get-tuple-element.720), channel_id=1, replica_groups=mesh['sec'=32,'blk'=8] {'sec','blk'}, use_global_device_ids=true, to_apply=%region_4.0 | all-reduce | flops 128 | bytes 1024 | tf_op jit(solution)/shard_map/psum | solution.py:121
  185.0 57.8 %all-reduce.23.cloned.1.call-done = (f32[128,128]{1,0:T(8,128)}, f32[1,128,128]{2,1,0:T(8,128)}) async-done(((f32[128,128]{1,0:T(8,128)}, f32[1,128,128]{2,1,0:T(8,128)}), (f32[128,128]{1,0:T(8,128)}, f32[1,128,128]{2,1,0:T(8,128)})) %all-reduce.23.cloned.1.call-update) | async-done | bytes 131088 | tf_op jit(solution)/shard_map/psum | solution.py:82
  244.9 75.7 %all-gather.12.cloned.1.call-done = f32[4096,128]{1,0:T(8,128)} async-done(((f32[128,128]{1,0:T(8,128)}), f32[4096,128]{1,0:T(8,128)}) %all-gather.12.cloned.1.call-update) | async-done | bytes 2097168 | tf_op jit(solution)/shard_map/all_gather | solution.py:25
  320.6 77.6 %all-gather.6.cloned.1.call-done = f32[32,128,128]{2,1,0:T(8,128)} async-done(((f32[1,128,128]{2,1,0:T(8,128)}), f32[32,128,128]{2,1,0:T(8,128)}) %all-gather.6.cloned.1.call-update) | async-done | bytes 2097168 | tf_op jit(solution)/shard_map/all_gather | solution.py:25
  398.3 63.2 %while.64 = (s32[]{:T(128)}, f32[128,128]{0,1:T(8,128)S(1)}, s32[]{:T(128)}, f32[32,128,128]{2,1,0:T(8,128)}, f32[32,128,128]{2,1,0:T(8,128)}, /*index=5*/s32[]{:T(128)}, s32[]{:T(128)}) while((s32[]{:T(128)}, f32[128,128]{0,1:T(8,128)S(1)}, s32[]{:T(128)}, f32[32,128,128]{2,1,0:T(8,128)}, f32[32,128,128]{2,1,0:T(8,128)}, ...), condition=%wide.region_8.9_spmd.clone, body=%wide.region_7.8_spmd.clone.sunk | while | flops 25231364 | bytes 723043 | solution.py:34
  461.8 17.8 %all_gather.59 = bf16[128,2048]{1,0:T(8,128)(2,1)S(1)} all-gather(bf16[128,256]{1,0:T(8,128)(2,1)S(1)} %get-tuple-element.722), channel_id=1, replica_groups=mesh['sec'=32,'blk'=8] {'blk'}, dimensions={1}, use_global_device_ids=true | all-gather | bytes 589824 | tf_op jit(solution)/shard_map/all_gather | solution.py:101
  480.8 57.6 %all-reduce.13.cloned.1.call-done = f32[1,128,128]{2,1,0:T(8,128)} async-done(((f32[1,128,128]{2,1,0:T(8,128)}), f32[1,128,128]{2,1,0:T(8,128)}) %all-reduce.13.cloned.1.call-update) | async-done | bytes 65552 | tf_op jit(solution)/shard_map/psum | solution.py:103
  549.1 83.2 %psum.110 = f32[1,128]{1,0:T(1,128)S(1)} all-reduce(f32[1,128]{1,0:T(1,128)S(1)} %bitcast.287), channel_id=1, replica_groups=mesh['sec'=32,'blk'=8] {'sec','blk'}, use_global_device_ids=true, to_apply=%region_11.12 | all-reduce | flops 128 | bytes 1024 | tf_op jit(solution)/shard_map/psum | solution.py:149
  632.5 72.3 %psum.111 = f32[128]{0:T(128)S(1)} all-reduce(f32[128]{0:T(128)S(1)} %get-tuple-element.687), channel_id=1, replica_groups=mesh['sec'=32,'blk'=8] {'sec','blk'}, use_global_device_ids=true, to_apply=%region_13.14 | all-reduce | flops 128 | bytes 1024 | tf_op jit(solution)/shard_map/psum | solution.py:121
  720.1 58.5 %all-reduce.15.cloned.1.call-done = f32[1,128,128]{2,1,0:T(8,128)} async-done(((f32[1,128,128]{2,1,0:T(8,128)}), f32[1,128,128]{2,1,0:T(8,128)}) %all-reduce.15.cloned.1.call-update) | async-done | bytes 65552 | tf_op jit(solution)/shard_map/psum | solution.py:138
  778.7 77.7 %all-gather.8.cloned.1.call-done = f32[32,128,128]{2,1,0:T(8,128)} async-done(((f32[1,128,128]{2,1,0:T(8,128)}), f32[32,128,128]{2,1,0:T(8,128)}) %all-gather.8.cloned.1.call-update) | async-done | bytes 2097168 | tf_op jit(solution)/shard_map/all_gather | solution.py:25
  856.4 63.2 %while.65 = (s32[]{:T(128)}, f32[128,128]{0,1:T(8,128)S(1)}, s32[]{:T(128)}, f32[32,128,128]{2,1,0:T(8,128)}, f32[32,128,128]{2,1,0:T(8,128)}, /*index=5*/s32[]{:T(128)}, s32[]{:T(128)}) while((s32[]{:T(128)}, f32[128,128]{0,1:T(8,128)S(1)}, s32[]{:T(128)}, f32[32,128,128]{2,1,0:T(8,128)}, f32[32,128,128]{2,1,0:T(8,128)}, ...), condition=%wide.region_16.17_spmd.clone, body=%wide.region_15.16_spmd.clone.sunk | while | flops 25231364 | bytes 723043 | solution.py:34
  920.6 17.8 %all_gather.63 = bf16[128,2048]{1,0:T(8,128)(2,1)S(1)} all-gather(bf16[128,256]{1,0:T(8,128)(2,1)S(1)} %get-tuple-element.724), channel_id=1, replica_groups=mesh['sec'=32,'blk'=8] {'blk'}, dimensions={1}, use_global_device_ids=true | all-gather | bytes 589824 | tf_op jit(solution)/shard_map/all_gather | solution.py:101
  939.7 57.4 %all-reduce.17.cloned.1.call-done = f32[1,128,128]{2,1,0:T(8,128)} async-done(((f32[1,128,128]{2,1,0:T(8,128)}), f32[1,128,128]{2,1,0:T(8,128)}) %all-reduce.17.cloned.1.call-update) | async-done | bytes 65552 | tf_op jit(solution)/shard_map/psum | solution.py:103
  1007.8 83.2 %psum.114 = f32[2,128]{1,0:T(2,128)S(1)} all-reduce(f32[2,128]{1,0:T(2,128)S(1)} %multiply_reduce_fusion.3), channel_id=1, replica_groups=mesh['sec'=32,'blk'=8] {'sec','blk'}, use_global_device_ids=true, to_apply=%region_19.20 | all-reduce | flops 256 | bytes 2048 | tf_op jit(solution)/shard_map/psum | solution.py:149
  1091.2 72.3 %psum.115 = f32[128]{0:T(128)S(1)} all-reduce(f32[128]{0:T(128)S(1)} %get-tuple-element.683), channel_id=1, replica_groups=mesh['sec'=32,'blk'=8] {'sec','blk'}, use_global_device_ids=true, to_apply=%region_22.23 | all-reduce | flops 128 | bytes 1024 | tf_op jit(solution)/shard_map/psum | solution.py:121
  1178.8 58.5 %all-reduce.19.cloned.1.call-done = f32[1,128,128]{2,1,0:T(8,128)} async-done(((f32[1,128,128]{2,1,0:T(8,128)}), f32[1,128,128]{2,1,0:T(8,128)}) %all-reduce.19.cloned.1.call-update) | async-done | bytes 65552 | tf_op jit(solution)/shard_map/psum | solution.py:138
  1243.8 71.1 %all-gather.10.cloned.1.call-done = f32[32,128,128]{2,1,0:T(8,128)} async-done(((f32[1,128,128]{2,1,0:T(8,128)}), f32[32,128,128]{2,1,0:T(8,128)}) %all-gather.10.cloned.1.call-update) | async-done | bytes 2097168 | tf_op jit(solution)/shard_map/all_gather | solution.py:25
  1314.9 63.2 %while.66 = (s32[]{:T(128)}, f32[128,128]{0,1:T(8,128)S(1)}, s32[]{:T(128)}, f32[32,128,128]{2,1,0:T(8,128)}, f32[32,128,128]{2,1,0:T(8,128)}, /*index=5*/s32[]{:T(128)}, s32[]{:T(128)}) while((s32[]{:T(128)}, f32[128,128]{0,1:T(8,128)S(1)}, s32[]{:T(128)}, f32[32,128,128]{2,1,0:T(8,128)}, f32[32,128,128]{2,1,0:T(8,128)}, ...), condition=%wide.region_26.27_spmd.clone, body=%wide.region_25.26_spmd.clone.sunk | while | flops 25231364 | bytes 723043 | solution.py:34
  1379.1 17.8 %all_gather.67 = bf16[128,2048]{1,0:T(8,128)(2,1)S(1)} all-gather(bf16[128,256]{1,0:T(8,128)(2,1)S(1)} %get-tuple-element.726), channel_id=1, replica_groups=mesh['sec'=32,'blk'=8] {'blk'}, dimensions={1}, use_global_device_ids=true | all-gather | bytes 589824 | tf_op jit(solution)/shard_map/all_gather | solution.py:101
  1398.0 57.6 %all-reduce.21.cloned.1.call-done = f32[1,128,128]{2,1,0:T(8,128)} async-done(((f32[1,128,128]{2,1,0:T(8,128)}), f32[1,128,128]{2,1,0:T(8,128)}) %all-reduce.21.cloned.1.call-update) | async-done | bytes 65552 | tf_op jit(solution)/shard_map/psum | solution.py:103
  1467.2 83.2 %psum.118 = f32[3,128]{1,0:T(4,128)S(1)} all-reduce(f32[3,128]{1,0:T(4,128)S(1)} %multiply_reduce_fusion.1), channel_id=1, replica_groups=mesh['sec'=32,'blk'=8] {'sec','blk'}, use_global_device_ids=true, to_apply=%region_29.30 | all-reduce | flops 384 | bytes 3072 | tf_op jit(solution)/shard_map/psum | solution.py:149
  1550.6 72.3 %psum.119 = f32[128]{0:T(128)S(1)} all-reduce(f32[128]{0:T(128)S(1)} %multiply_reduce_fusion.4), channel_id=1, replica_groups=mesh['sec'=32,'blk'=8] {'sec','blk'}, use_global_device_ids=true, to_apply=%region_32.33 | all-reduce | flops 128 | bytes 1024 | tf_op jit(solution)/shard_map/psum | solution.py:121
  (529 shorter events, 334.7 us)
Async XLA Ops:
  6.5 68.7 %all-reduce.11.cloned.1.call-start = ((), (), s32[]{:S(2)}) async-start(), calls=%async_computation | async-start | bytes 131072 | tf_op jit(solution)/shard_map/psum | solution.py:103
  9.3 233.5 %all-reduce.23.cloned.1.call-start = ((), (), s32[]{:S(2)}) async-start(), calls=%async_computation.10 | async-start | bytes 262144 | tf_op jit(solution)/shard_map/psum | solution.py:82
  26.6 59.3 %copy-start.2 = (f32[128,256]{1,0:T(8,128)S(1)}, f32[128,256]{1,0:T(8,128)}, u32[]{:S(2)}) copy-start(f32[128,256]{1,0:T(8,128)} %param.58) | copy-start | bytes 393220
  26.6 59.3 %copy-start.8 = (f32[128,256]{1,0:T(8,128)S(1)}, f32[128,256]{1,0:T(8,128)}, u32[]{:S(2)}) copy-start(f32[128,256]{1,0:T(8,128)} %param.59) | copy-start | bytes 393220
  76.1 5.4 collective-permute-start
  80.2 5.7 collective-permute-start.1
  169.6 228.7 %copy-start.11 = (f32[128]{0:T(128)}, f32[128]{0:T(128)S(1)}, u32[]{:S(2)}) copy-start(f32[128]{0:T(128)S(1)} %psum.106) | copy-start | bytes 1540
  185.0 135.7 %all-gather.12.cloned.1.call-start = ((), (), s32[]{:S(2)}) async-start(), calls=%async_computation.9 | async-start | bytes 2162688 | tf_op jit(solution)/shard_map/all_gather | solution.py:25
  244.3 154.0 %all-gather.6.cloned.1.call-start = ((), (), s32[]{:S(2)}) async-start(), calls=%async_computation.1 | async-start | bytes 2162688 | tf_op jit(solution)/shard_map/all_gather | solution.py:25
  244.9 293.6 %all-reduce.13.cloned.1.call-start = ((), (), s32[]{:S(2)}) async-start(), calls=%async_computation.2 | async-start | bytes 131072 | tf_op jit(solution)/shard_map/psum | solution.py:103
  398.3 81.4 %copy-start.7 = (bf16[256,128]{1,0:T(8,128)(2,1)S(1)}, bf16[256,128]{1,0:T(8,128)(2,1)}, u32[]{:S(2)}) copy-start(bf16[256,128]{1,0:T(8,128)(2,1)} %param.64) | copy-start | bytes 196612
  480.4 298.2 %all-reduce.15.cloned.1.call-start = ((), (), s32[]{:S(2)}) async-start(), calls=%async_computation.3 | async-start | bytes 131072 | tf_op jit(solution)/shard_map/psum | solution.py:138
  539.3 4.9 collective-permute-start.2
  542.9 5.7 collective-permute-start.3
  720.0 136.3 %all-gather.8.cloned.1.call-start = ((), (), s32[]{:S(2)}) async-start(), calls=%async_computation.4 | async-start | bytes 2162688 | tf_op jit(solution)/shard_map/all_gather | solution.py:25
  778.6 218.5 %all-reduce.17.cloned.1.call-start = ((), (), s32[]{:S(2)}) async-start(), calls=%async_computation.5 | async-start | bytes 131072 | tf_op jit(solution)/shard_map/psum | solution.py:103
  939.1 298.2 %all-reduce.19.cloned.1.call-start = ((), (), s32[]{:S(2)}) async-start(), calls=%async_computation.6 | async-start | bytes 131072 | tf_op jit(solution)/shard_map/psum | solution.py:138
  998.0 4.9 collective-permute-start.4
  1001.6 5.7 collective-permute-start.5
  1178.8 136.2 %all-gather.10.cloned.1.call-start = ((), (), s32[]{:S(2)}) async-start(), calls=%async_computation.7 | async-start | bytes 2162688 | tf_op jit(solution)/shard_map/all_gather | solution.py:25
  1237.3 218.3 %all-reduce.21.cloned.1.call-start = ((), (), s32[]{:S(2)}) async-start(), calls=%async_computation.8 | async-start | bytes 131072 | tf_op jit(solution)/shard_map/psum | solution.py:103
  1456.6 175.3 %copy-start.5 = (f32[128,256]{1,0:T(8,128)S(1)}, f32[128,256]{1,0:T(8,128)}, u32[]{:S(2)}) copy-start(f32[128,256]{1,0:T(8,128)} %get-tuple-element.725) | copy-start | bytes 393220
  1456.6 5.0 collective-permute-start.6
  1460.3 5.7 collective-permute-start.7
  (7 other events, 206.9 us)
Sparse Core Ops, SparseCore 0:
  9.7 65.5 all-reduce.10
  185.1 57.6 all-reduce.22
  245.4 75.2 all-gather.11
  323.1 75.1 all-gather.5
  480.5 57.8 all-reduce.12
  720.2 58.4 all-reduce.14
  781.2 75.1 all-gather.7
  939.3 57.8 all-reduce.16
  1178.9 58.4 all-reduce.18
  1239.8 75.1 all-gather.9
  1397.8 57.8 all-reduce.20
where the time goes:
time: 1650 us; the launch traced here: 1640 us
  waiting for transfers between devices  702 us (43%)
  blocking collectives  674 us (41%)
  matrix products  116 us (7%)
  local copies, waits for them, and re-layouts  91.5 us (6%)
  other arithmetic  20.7 us (1%)
  starting transfers between devices  18.2 us (1%)
    all_gather x4, waiting for transfers between devices, entering(): pieces = jax.tree.map(lambda part: lax.all_gather(part, axis), value)  302 us
    psum x4, blocking collectives, lengths(): lax.psum(jnp.sum(vector * vector, axis=1), ('sec', 'blk')) + epsilon  300 us
    psum x3, blocking collectives, local(): lax.psum(jnp.sum(product[None] * stacked, axis=2), ('sec', 'blk'))  250 us
    psum x4, waiting for transfers between devices, operator(): lax.psum(jnp.dot(rounded, ahead_panel, preferred_element_type=jnp.float32...  207 us
    psum x2, waiting for transfers between devices, local(): lax.psum(jnp.dot(precondition_folded, selector, precision=highest), 'blk')  117 us
    dot_general x93, matrix products, compose(): jnp.dot(first_value, second_map.T, precision=highest) + second_value  97.7 us
    dynamic_slice x186, local copies, waits for them, and re-layouts, step(): longer = join(so_far, jax.tree.map(lambda part: part[position], pieces))  87 us
    all_gather x4, blocking collectives, operator(): lax.all_gather(rounded, 'blk', axis=1, tiled=True)  69.6 us
  transfers between devices with their start and end apart: 19, of which 15 were waited for; matrix products, arithmetic and copies ran while one was open for 1% of the time, Pallas kernels for 0%

commit v1 on v0

--- a/solution.py
+++ b/solution.py
@@ -5,6 +5,19 @@
 
 KRYLOV = 3
 epsilon = 1e-06
+
+
+def gather_around(x, axis, dim):
+    ways = lax.axis_size(axis)
+    up = [(d, (d + 1) % ways) for d in range(ways)]
+    down = [(d, (d - 1) % ways) for d in range(ways)]
+    earlier, later = ([x], [x])
+    for _ in range(ways // 2):
+        earlier.append(lax.ppermute(earlier[-1], axis, up))
+    for _ in range((ways - 1) // 2):
+        later.append(lax.ppermute(later[-1], axis, down))
+    line = jnp.concatenate([*earlier[::-1], *later[1:]], axis=dim)
+    return jnp.roll(line, (lax.axis_index(axis) - ways // 2) * x.shape[dim], axis=dim)
 
 
 def extended(x, sides, width):
@@ -130,7 +143,7 @@
     for column in range(KRYLOV):
         precondition_rounded = basis[column].astype(jnp.bfloat16)
         precondition_folded = lax.dot_general(
-            lax.all_gather(precondition_rounded, "blk", axis=1, tiled=True),
+            gather_around(precondition_rounded, "blk", 1),
             block_inverse,
             contract,
             preferred_element_type=jnp.float32,

time: 1650 us -> 1680 us (1.018)
  waiting for transfers between devices: 702 us -> 743 us
  blocking collectives: 674 us -> 635 us
  starting transfers between devices: 18.2 us -> 48.9 us
    all_gather x3 -> x0, blocking collectives: 41.1 us -> none  [local(): lax.all_gather(precondition_rounded, 'blk', axis=1, tiled=True)]
    ppermute x0 -> x21, starting transfers between devices: none -> 30.7 us  [the longest x12 18.6 us: gather_around(): earlier.append(lax.ppermute(earlier[-1], axis, up))]
  transfers between devices with their start and end apart: 19 -> 40, of which waited for: 15 -> 29; matrix products, arithmetic and copies ran while one was open for 1% -> 1% of each run, Pallas kernels for 0% -> 0%
where the time goes in v1:
time: 1680 us; the launch traced here: 1670 us
  waiting for transfers between devices  743 us (44%)
  blocking collectives  635 us (38%)
  matrix products  117 us (7%)
  local copies, waits for them, and re-layouts  91.9 us (5%)
  starting transfers between devices  48.9 us (3%)
  other arithmetic  20.3 us (1%)
    all_gather x4, waiting for transfers between devices, entering(): pieces = jax.tree.map(lambda part: lax.all_gather(part, axis), value)  302 us
    psum x4, blocking collectives, lengths(): lax.psum(jnp.sum(vector * vector, axis=1), ('sec', 'blk')) + epsilon  300 us
    psum x3, blocking collectives, local(): lax.psum(jnp.sum(product[None] * stacked, axis=2), ('sec', 'blk'))  250 us
    psum x4, waiting for transfers between devices, operator(): lax.psum(jnp.dot(rounded, ahead_panel, preferred_element_type=jnp.float32...  220 us
    psum x2, waiting for transfers between devices, local(): lax.psum(jnp.dot(precondition_folded, selector, precision=highest), 'blk')  128 us
    dot_general x93, matrix products, compose(): jnp.dot(first_value, second_map.T, precision=highest) + second_value  97.7 us
    dynamic_slice x186, local copies, waits for them, and re-layouts, step(): longer = join(so_far, jax.tree.map(lambda part: part[position], pieces))  87 us
    all_gather x4, blocking collectives, operator(): lax.all_gather(rounded, 'blk', axis=1, tiled=True)  69.6 us
  transfers between devices with their start and end apart: 40, of which 29 were waited for; matrix products, arithmetic and copies ran while one was open for 1% of the time, Pallas kernels for 0%

profile of v1, /device:TPU:1, one launch (start us, length us, event | category | flops | bytes accessed | tf_op | source)
XLA Modules:
  0.0 1674.0 jit_solution(3170806978275346151)
XLA Ops:
  27.7 47.5 %all-reduce.11.cloned.1.call-done = f32[1,128,128]{1,2,0:T(8,128)} async-done(((f32[1,128,128]{1,2,0:T(8,128)}), f32[1,128,128]{1,2,0:T(8,128)}) %all-reduce.11.cloned.1.call-update) | async-done | bytes 65552 | tf_op jit(solution)/shard_map/psum | solution.py:116
  85.3 83.2 %psum.106 = f32[128]{0:T(128)S(1)} all-reduce(f32[128]{0:T(128)S(1)} %get-tuple-element.721), channel_id=1, replica_groups=mesh['sec'=32,'blk'=8] {'sec','blk'}, use_global_device_ids=true, to_apply=%region_4.5 | all-reduce | flops 128 | bytes 1024 | tf_op jit(solution)/shard_map/psum | solution.py:134
  200.4 59.6 %all-reduce.23.cloned.1.call-done = (f32[128,128]{1,0:T(8,128)}, f32[1,128,128]{2,1,0:T(8,128)}) async-done(((f32[128,128]{1,0:T(8,128)}, f32[1,128,128]{2,1,0:T(8,128)}), (f32[128,128]{1,0:T(8,128)}, f32[1,128,128]{2,1,0:T(8,128)})) %all-reduce.23.cloned.1.call-update) | async-done | bytes 131088 | tf_op jit(solution)/shard_map/psum | solution.py:95
  262.2 75.7 %all-gather.12.cloned.1.call-done = f32[4096,128]{1,0:T(8,128)} async-done(((f32[128,128]{1,0:T(8,128)}), f32[4096,128]{1,0:T(8,128)}) %all-gather.12.cloned.1.call-update) | async-done | bytes 2097168 | tf_op jit(solution)/shard_map/all_gather | solution.py:38
  337.9 77.6 %all-gather.6.cloned.1.call-done = f32[32,128,128]{2,1,0:T(8,128)} async-done(((f32[1,128,128]{2,1,0:T(8,128)}), f32[32,128,128]{2,1,0:T(8,128)}) %all-gather.6.cloned.1.call-update) | async-done | bytes 2097168 | tf_op jit(solution)/shard_map/all_gather | solution.py:38
  415.5 63.2 %while.64 = (s32[]{:T(128)}, f32[128,128]{0,1:T(8,128)S(1)}, s32[]{:T(128)}, f32[32,128,128]{2,1,0:T(8,128)}, f32[32,128,128]{2,1,0:T(8,128)}, /*index=5*/s32[]{:T(128)}, s32[]{:T(128)}) while((s32[]{:T(128)}, f32[128,128]{0,1:T(8,128)S(1)}, s32[]{:T(128)}, f32[32,128,128]{2,1,0:T(8,128)}, f32[32,128,128]{2,1,0:T(8,128)}, ...), condition=%wide.region_8.10_spmd.clone, body=%wide.region_7.9_spmd.clone.sunk | while | flops 25231364 | bytes 723043 | solution.py:47
  479.1 17.8 %all_gather.49 = bf16[128,2048]{1,0:T(8,128)(2,1)S(1)} all-gather(bf16[128,256]{1,0:T(8,128)(2,1)S(1)} %get-tuple-element.723), channel_id=1, replica_groups=mesh['sec'=32,'blk'=8] {'blk'}, dimensions={1}, use_global_device_ids=true | all-gather | bytes 589824 | tf_op jit(solution)/shard_map/all_gather | solution.py:114
  498.1 57.6 %all-reduce.13.cloned.1.call-done = f32[1,128,128]{2,1,0:T(8,128)} async-done(((f32[1,128,128]{2,1,0:T(8,128)}), f32[1,128,128]{2,1,0:T(8,128)}) %all-reduce.13.cloned.1.call-update) | async-done | bytes 65552 | tf_op jit(solution)/shard_map/psum | solution.py:116
  566.4 83.2 %psum.110 = f32[1,128]{1,0:T(1,128)S(1)} all-reduce(f32[1,128]{1,0:T(1,128)S(1)} %bitcast.284), channel_id=1, replica_groups=mesh['sec'=32,'blk'=8] {'sec','blk'}, use_global_device_ids=true, to_apply=%region_11.13 | all-reduce | flops 128 | bytes 1024 | tf_op jit(solution)/shard_map/psum | solution.py:162
  649.8 72.3 %psum.111 = f32[128]{0:T(128)S(1)} all-reduce(f32[128]{0:T(128)S(1)} %get-tuple-element.688), channel_id=1, replica_groups=mesh['sec'=32,'blk'=8] {'sec','blk'}, use_global_device_ids=true, to_apply=%region_13.15 | all-reduce | flops 128 | bytes 1024 | tf_op jit(solution)/shard_map/psum | solution.py:134
  740.1 63.9 %all-reduce.15.cloned.1.call-done = f32[1,128,128]{2,1,0:T(8,128)} async-done(((f32[1,128,128]{2,1,0:T(8,128)}), f32[1,128,128]{2,1,0:T(8,128)}) %all-reduce.15.cloned.1.call-update) | async-done | bytes 65552 | tf_op jit(solution)/shard_map/psum | solution.py:151
  804.1 77.7 %all-gather.8.cloned.1.call-done = f32[32,128,128]{2,1,0:T(8,128)} async-done(((f32[1,128,128]{2,1,0:T(8,128)}), f32[32,128,128]{2,1,0:T(8,128)}) %all-gather.8.cloned.1.call-update) | async-done | bytes 2097168 | tf_op jit(solution)/shard_map/all_gather | solution.py:38
  881.7 63.2 %while.65 = (s32[]{:T(128)}, f32[128,128]{0,1:T(8,128)S(1)}, s32[]{:T(128)}, f32[32,128,128]{2,1,0:T(8,128)}, f32[32,128,128]{2,1,0:T(8,128)}, /*index=5*/s32[]{:T(128)}, s32[]{:T(128)}) while((s32[]{:T(128)}, f32[128,128]{0,1:T(8,128)S(1)}, s32[]{:T(128)}, f32[32,128,128]{2,1,0:T(8,128)}, f32[32,128,128]{2,1,0:T(8,128)}, ...), condition=%wide.region_16.18_spmd.clone, body=%wide.region_15.17_spmd.clone.sunk | while | flops 25231364 | bytes 723043 | solution.py:47
  945.9 17.8 %all_gather.52 = bf16[128,2048]{1,0:T(8,128)(2,1)S(1)} all-gather(bf16[128,256]{1,0:T(8,128)(2,1)S(1)} %get-tuple-element.725), channel_id=1, replica_groups=mesh['sec'=32,'blk'=8] {'blk'}, dimensions={1}, use_global_device_ids=true | all-gather | bytes 589824 | tf_op jit(solution)/shard_map/all_gather | solution.py:114
  964.9 57.6 %all-reduce.17.cloned.1.call-done = f32[1,128,128]{2,1,0:T(8,128)} async-done(((f32[1,128,128]{2,1,0:T(8,128)}), f32[1,128,128]{2,1,0:T(8,128)}) %all-reduce.17.cloned.1.call-update) | async-done | bytes 65552 | tf_op jit(solution)/shard_map/psum | solution.py:116
  1033.3 83.2 %psum.114 = f32[2,128]{1,0:T(2,128)S(1)} all-reduce(f32[2,128]{1,0:T(2,128)S(1)} %multiply_reduce_fusion.3), channel_id=1, replica_groups=mesh['sec'=32,'blk'=8] {'sec','blk'}, use_global_device_ids=true, to_apply=%region_19.21 | all-reduce | flops 256 | bytes 2048 | tf_op jit(solution)/shard_map/psum | solution.py:162
  1116.8 72.3 %psum.115 = f32[128]{0:T(128)S(1)} all-reduce(f32[128]{0:T(128)S(1)} %get-tuple-element.684), channel_id=1, replica_groups=mesh['sec'=32,'blk'=8] {'sec','blk'}, use_global_device_ids=true, to_apply=%region_22.24 | all-reduce | flops 128 | bytes 1024 | tf_op jit(solution)/shard_map/psum | solution.py:134
  1207.1 63.9 %all-reduce.19.cloned.1.call-done = f32[1,128,128]{2,1,0:T(8,128)} async-done(((f32[1,128,128]{2,1,0:T(8,128)}), f32[1,128,128]{2,1,0:T(8,128)}) %all-reduce.19.cloned.1.call-update) | async-done | bytes 65552 | tf_op jit(solution)/shard_map/psum | solution.py:151
  1277.3 71.3 %all-gather.10.cloned.1.call-done = f32[32,128,128]{2,1,0:T(8,128)} async-done(((f32[1,128,128]{2,1,0:T(8,128)}), f32[32,128,128]{2,1,0:T(8,128)}) %all-gather.10.cloned.1.call-update) | async-done | bytes 2097168 | tf_op jit(solution)/shard_map/all_gather | solution.py:38
  1348.6 63.2 %while.66 = (s32[]{:T(128)}, f32[128,128]{0,1:T(8,128)S(1)}, s32[]{:T(128)}, f32[32,128,128]{2,1,0:T(8,128)}, f32[32,128,128]{2,1,0:T(8,128)}, /*index=5*/s32[]{:T(128)}, s32[]{:T(128)}) while((s32[]{:T(128)}, f32[128,128]{0,1:T(8,128)S(1)}, s32[]{:T(128)}, f32[32,128,128]{2,1,0:T(8,128)}, f32[32,128,128]{2,1,0:T(8,128)}, ...), condition=%wide.region_26.28_spmd.clone, body=%wide.region_25.27_spmd.clone.sunk | while | flops 25231364 | bytes 723043 | solution.py:47
  1412.8 17.8 %all_gather.55 = bf16[128,2048]{1,0:T(8,128)(2,1)S(1)} all-gather(bf16[128,256]{1,0:T(8,128)(2,1)S(1)} %get-tuple-element.727), channel_id=1, replica_groups=mesh['sec'=32,'blk'=8] {'blk'}, dimensions={1}, use_global_device_ids=true | all-gather | bytes 589824 | tf_op jit(solution)/shard_map/all_gather | solution.py:114
  1431.8 57.6 %all-reduce.21.cloned.1.call-done = f32[1,128,128]{2,1,0:T(8,128)} async-done(((f32[1,128,128]{2,1,0:T(8,128)}), f32[1,128,128]{2,1,0:T(8,128)}) %all-reduce.21.cloned.1.call-update) | async-done | bytes 65552 | tf_op jit(solution)/shard_map/psum | solution.py:116
  1500.9 83.2 %psum.118 = f32[3,128]{1,0:T(4,128)S(1)} all-reduce(f32[3,128]{1,0:T(4,128)S(1)} %multiply_reduce_fusion.1), channel_id=1, replica_groups=mesh['sec'=32,'blk'=8] {'sec','blk'}, use_global_device_ids=true, to_apply=%region_29.31 | all-reduce | flops 384 | bytes 3072 | tf_op jit(solution)/shard_map/psum | solution.py:162
  1584.3 72.3 %psum.119 = f32[128]{0:T(128)S(1)} all-reduce(f32[128]{0:T(128)S(1)} %multiply_reduce_fusion.4), channel_id=1, replica_groups=mesh['sec'=32,'blk'=8] {'sec','blk'}, use_global_device_ids=true, to_apply=%region_32.34 | all-reduce | flops 128 | bytes 1024 | tf_op jit(solution)/shard_map/psum | solution.py:134
  (591 shorter events, 342.4 us)
Async XLA Ops:
  6.5 68.6 %all-reduce.11.cloned.1.call-start = ((), (), s32[]{:S(2)}) async-start(), calls=%async_computation | async-start | bytes 131072 | tf_op jit(solution)/shard_map/psum | solution.py:116
  9.3 250.7 %all-reduce.23.cloned.1.call-start = ((), (), s32[]{:S(2)}) async-start(), calls=%async_computation.10 | async-start | bytes 262144 | tf_op jit(solution)/shard_map/psum | solution.py:95
  76.1 4.4 collective-permute-start
  79.1 5.7 collective-permute-start.1
  170.3 17.4 %collective-permute-start.3 = (bf16[128,256]{1,0:T(8,128)(2,1)S(1)}, bf16[128,256]{1,0:T(8,128)(2,1)S(1)}, u32[]{:S(2)}, u32[]{:S(2)}) collective-permute-start(bf16[128,256]{1,0:T(8,128)(2,1)S(1)} %collective-permute-done.2), channel_id=1, source_target_pairs={{0,1},{1,2},{2,3},{3,4},{4,5},{5,6},{6,7},{7,0},{8,9},{9,10},{10,1... | collective-permute-start | bytes 196616 | tf_op jit(solution)/shard_map/ppermute | solution.py:16
  200.4 137.5 %all-gather.12.cloned.1.call-start = ((), (), s32[]{:S(2)}) async-start(), calls=%async_computation.9 | async-start | bytes 2162688 | tf_op jit(solution)/shard_map/all_gather | solution.py:38
  261.5 154.0 %all-gather.6.cloned.1.call-start = ((), (), s32[]{:S(2)}) async-start(), calls=%async_computation.1 | async-start | bytes 2162688 | tf_op jit(solution)/shard_map/all_gather | solution.py:38
  262.1 293.6 %all-reduce.13.cloned.1.call-start = ((), (), s32[]{:S(2)}) async-start(), calls=%async_computation.2 | async-start | bytes 131072 | tf_op jit(solution)/shard_map/psum | solution.py:116
  497.7 306.3 %all-reduce.15.cloned.1.call-start = ((), (), s32[]{:S(2)}) async-start(), calls=%async_computation.3 | async-start | bytes 131072 | tf_op jit(solution)/shard_map/psum | solution.py:151
  556.6 4.9 collective-permute-start.9
  560.1 5.7 collective-permute-start.10
  728.5 4.9 collective-permute-start.13
  733.4 4.9 collective-permute-start.14
  740.0 141.7 %all-gather.8.cloned.1.call-start = ((), (), s32[]{:S(2)}) async-start(), calls=%async_computation.4 | async-start | bytes 2162688 | tf_op jit(solution)/shard_map/all_gather | solution.py:38
  804.0 218.5 %all-reduce.17.cloned.1.call-start = ((), (), s32[]{:S(2)}) async-start(), calls=%async_computation.5 | async-start | bytes 131072 | tf_op jit(solution)/shard_map/psum | solution.py:116
  964.5 306.5 %all-reduce.19.cloned.1.call-start = ((), (), s32[]{:S(2)}) async-start(), calls=%async_computation.6 | async-start | bytes 131072 | tf_op jit(solution)/shard_map/psum | solution.py:151
  1023.4 5.1 collective-permute-start.18
  1027.2 5.7 collective-permute-start.19
  1195.5 4.9 collective-permute-start.22
  1200.4 4.9 collective-permute-start.23
  1207.0 141.6 %all-gather.10.cloned.1.call-start = ((), (), s32[]{:S(2)}) async-start(), calls=%async_computation.7 | async-start | bytes 2162688 | tf_op jit(solution)/shard_map/all_gather | solution.py:38
  1271.0 218.3 %all-reduce.21.cloned.1.call-start = ((), (), s32[]{:S(2)}) async-start(), calls=%async_computation.8 | async-start | bytes 131072 | tf_op jit(solution)/shard_map/psum | solution.py:116
  1490.3 5.0 collective-permute-start.27
  1494.0 5.7 collective-permute-start.28
  (28 other events, 954.9 us)
Sparse Core Ops, SparseCore 0:
  9.7 65.4 all-reduce.10
  200.5 59.4 all-reduce.22
  262.6 75.2 all-gather.11
  340.3 75.1 all-gather.5
  497.8 57.8 all-reduce.12
  740.2 63.7 all-reduce.14
  806.6 75.1 all-gather.7
  964.6 57.8 all-reduce.16
  1207.2 63.8 all-reduce.18
  1273.5 75.1 all-gather.9
  1431.5 57.8 all-reduce.20
